TPU v7x, 32 devices: a whole 2x2x4 slice. The times are simulated.
32 devices in a mesh: cp: 4 (over y, x), fsdp: 2 (over core), rep: 4 (over z).
Axes of the slice: x: 2, y: 2, z: 4, core: 2. Of those that a mesh axis runs over, the one named last changes fastest.
Arguments:
- tokens: bfloat16 [16, 2048, 768], P(('fsdp', 'rep'), 'cp'), may hold values from -6 to 6
- segments: int32 [16, 2048], P(('fsdp', 'rep')), may hold values from 0 to 3, never falling along the last dimension, each value on 1 to 1024 neighbouring positions
- g_one: bfloat16 [768], P('fsdp'), may hold values from 0.099609375 to 1.8984375
- b_one: bfloat16 [768], P('fsdp'), may hold values from -3 to 3
- w_qkv: bfloat16 [768, 2304], P('fsdp'), may hold values from -0.21875 to 0.21875
- b_query: bfloat16 [768], P('fsdp'), may hold values from -3 to 3
- b_value: bfloat16 [768], P('fsdp'), may hold values from -3 to 3
- w_out: bfloat16 [768, 768], P('fsdp'), may hold values from -1.75 to 1.75
- b_out: bfloat16 [768], P('fsdp'), may hold values from -3 to 3
- g_two: bfloat16 [768], P('fsdp'), may hold values from 0.099609375 to 1.8984375
- b_two: bfloat16 [768], P('fsdp'), may hold values from -3 to 3
- w_fc: bfloat16 [768, 3072], P('fsdp'), may hold values from -0.21875 to 0.21875
- b_fc: bfloat16 [3072], P('fsdp'), may hold values from -3 to 3
- w_proj: bfloat16 [3072, 768], P('fsdp'), may hold values from -0.109375 to 0.109375
- b_proj: bfloat16 [768], P('fsdp'), may hold values from -3 to 3
- cotangent: bfloat16 [16, 2048, 768], P(('fsdp', 'rep'), 'cp'), may hold values from -6 to 6
Outputs:
- layer_out: bfloat16 [16, 2048, 768], P(('fsdp', 'rep'), 'cp')
- tokens_grad: bfloat16 [16, 2048, 768], P(('fsdp', 'rep'), 'cp')
- dg_one: float32 [768], P('fsdp')
- db_one: float32 [768], P('fsdp')
- dw_qkv: float32 [768, 2304], P('fsdp')
- db_query: float32 [768], P('fsdp')
- db_value: float32 [768], P('fsdp')
- dw_out: float32 [768, 768], P('fsdp')
- db_out: float32 [768], P('fsdp')
- dg_two: float32 [768], P('fsdp')
- db_two: float32 [768], P('fsdp')
- dw_fc: float32 [768, 3072], P('fsdp')
- db_fc: float32 [3072], P('fsdp')
- dw_proj: float32 [3072, 768], P('fsdp')
- db_proj: float32 [768], P('fsdp')
Inputs may be any that keep to these rules, and one draw needn't show every extreme that they name: `segments`: in each sequence the ids never fall, and each document holds 1 to 1024 positions, one document exactly that many.
All inputs are finite; a program needn't handle non-finite values.
Results may differ from a plain program's by a relative error of at most 0.012.
The roundings to bfloat16 on the way count: a program that leaves them out, or rounds other values in their place, can miss the bound.
Values may be sent and summed in bfloat16 or wider, within the bound.
A program may use at most 384 MiB of HBM per device.

v0:
```python
import jax
import jax.numpy as jnp
from jax import lax
from jax.sharding import PartitionSpec as P

HEADS = 12


def layer_norm(value, gain, shift):
    center = value - jnp.mean(value, axis=-1, keepdims=True)
    spread = jnp.mean(center * center, axis=-1, keepdims=True)
    return center * lax.rsqrt(spread + 1e-05) * gain + shift


def gelu_tanh(value):
    return (
        0.5
        * value
        * (1.0 + jnp.tanh(0.7978845608028654 * (value + 0.044715 * value * value * value)))
    )


def inner_rows(left, right):
    return lax.dot_general(
        left, right, (((0,), (0,)), ((), ())), preferred_element_type=jnp.float32
    )


def times_trans(left, right):
    return lax.dot_general(
        left, right, (((1,), (1,)), ((), ())), preferred_element_type=jnp.float32
    )


def body(
    tokens,
    segments,
    g_one,
    b_one,
    w_qkv,
    b_query,
    b_value,
    w_out,
    b_out,
    g_two,
    b_two,
    w_fc,
    b_fc,
    w_proj,
    b_proj,
    cotangent,
):
    seqs, span, width = tokens.shape
    seq_len = segments.shape[1]
    rows = seqs * span
    size = width // HEADS
    scale = size ** (-0.5)
    first_pos = lax.axis_index("cp") * span
    full = (
        lax.all_gather(g_one, "fsdp", axis=0, tiled=True),
        lax.all_gather(b_one, "fsdp", axis=0, tiled=True),
        lax.all_gather(w_qkv, "fsdp", axis=0, tiled=True),
        lax.all_gather(b_query, "fsdp", axis=0, tiled=True),
        lax.all_gather(b_value, "fsdp", axis=0, tiled=True),
        lax.all_gather(w_out, "fsdp", axis=0, tiled=True),
        lax.all_gather(b_out, "fsdp", axis=0, tiled=True),
        lax.all_gather(g_two, "fsdp", axis=0, tiled=True),
        lax.all_gather(b_two, "fsdp", axis=0, tiled=True),
        lax.all_gather(w_fc, "fsdp", axis=0, tiled=True),
        lax.all_gather(b_fc, "fsdp", axis=0, tiled=True),
        lax.all_gather(w_proj, "fsdp", axis=0, tiled=True),
        lax.all_gather(b_proj, "fsdp", axis=0, tiled=True),
    )
    gain_one = full[0].astype(jnp.float32)
    shift_one = full[1].astype(jnp.float32)
    gain_two = full[7].astype(jnp.float32)
    shift_two = full[8].astype(jnp.float32)
    tok_rows = tokens.reshape(rows, width).astype(jnp.float32)
    normed = layer_norm(tok_rows, gain_one, shift_one).astype(jnp.bfloat16)
    qkv_bias = jnp.concatenate([full[3], jnp.zeros_like(full[3]), full[4]]).astype(jnp.float32)
    merged = (jnp.dot(normed, full[2], preferred_element_type=jnp.float32) + qkv_bias).astype(
        jnp.bfloat16
    )
    merged = merged.reshape(seqs, span, 3 * width)
    query = merged[:, :, :width]
    key_loc = merged[:, :, width : 2 * width]
    value_loc = merged[:, :, 2 * width :]
    keys_all, values_all = (
        lax.all_gather(key_loc, "cp", axis=1, tiled=True),
        lax.all_gather(value_loc, "cp", axis=1, tiled=True),
    )
    key_pos = jnp.arange(seq_len)

    def masked_scores(q_rows, k_rows, seq_ids, near_ids):
        length = k_rows.shape[0]
        q_three = q_rows.reshape(span, HEADS, size)
        k_three = k_rows.reshape(length, HEADS, size)
        scores = (
            jnp.einsum("qhd,khd->hqk", q_three, k_three, preferred_element_type=jnp.float32) * scale
        )
        query_ids = lax.dynamic_slice_in_dim(seq_ids, first_pos, span)
        query_pos = first_pos + jnp.arange(span)
        allowed = (query_ids[:, None] == near_ids[None, :]) & (
            key_pos[None, :] <= query_pos[:, None]
        )
        return jnp.where(allowed[None], scores, -1e30)

    def attend(item):
        q_rows, k_rows, v_rows, seq_ids, near_ids = item
        length = k_rows.shape[0]
        scores = masked_scores(q_rows, k_rows, seq_ids, near_ids)
        top = jnp.max(scores, axis=-1, keepdims=True)
        expo = jnp.exp(scores - top)
        total = jnp.sum(expo, axis=-1, keepdims=True)
        probs = (expo / total).astype(jnp.bfloat16)
        mixed = jnp.einsum(
            "hqk,khd->qhd",
            probs,
            v_rows.reshape(length, HEADS, size),
            preferred_element_type=jnp.float32,
        )
        return (
            mixed.reshape(span, width).astype(jnp.bfloat16),
            top[..., 0] + jnp.log(total[..., 0]),
        )

    mixed, log_total = lax.map(attend, (query, keys_all, values_all, segments, segments))
    mixed_rows = mixed.reshape(rows, width)
    branch = jnp.dot(mixed_rows, full[5], preferred_element_type=jnp.float32) + full[6].astype(
        jnp.float32
    )
    resid = tok_rows + branch
    normed_two = layer_norm(resid, gain_two, shift_two).astype(jnp.bfloat16)
    hidden = jnp.dot(normed_two, full[9], preferred_element_type=jnp.float32) + full[10].astype(
        jnp.float32
    )
    active = gelu_tanh(hidden).astype(jnp.bfloat16)
    output = jnp.dot(active, full[11], preferred_element_type=jnp.float32) + full[12].astype(
        jnp.float32
    )
    layer_out = (resid + output).astype(jnp.bfloat16).reshape(seqs, span, width)
    back = (
        lax.all_gather(g_one, "fsdp", axis=0, tiled=True),
        lax.all_gather(b_one, "fsdp", axis=0, tiled=True),
        lax.all_gather(w_qkv, "fsdp", axis=0, tiled=True),
        lax.all_gather(b_query, "fsdp", axis=0, tiled=True),
        lax.all_gather(b_value, "fsdp", axis=0, tiled=True),
        lax.all_gather(w_out, "fsdp", axis=0, tiled=True),
        lax.all_gather(b_out, "fsdp", axis=0, tiled=True),
        lax.all_gather(g_two, "fsdp", axis=0, tiled=True),
        lax.all_gather(b_two, "fsdp", axis=0, tiled=True),
        lax.all_gather(w_fc, "fsdp", axis=0, tiled=True),
        lax.all_gather(b_fc, "fsdp", axis=0, tiled=True),
        lax.all_gather(w_proj, "fsdp", axis=0, tiled=True),
        lax.all_gather(b_proj, "fsdp", axis=0, tiled=True),
    )
    keys_b, values_b = (
        lax.all_gather(key_loc, "cp", axis=1, tiled=True),
        lax.all_gather(value_loc, "cp", axis=1, tiled=True),
    )
    out_grad = cotangent.reshape(rows, width).astype(jnp.float32)
    d_output = out_grad.astype(jnp.bfloat16)
    dw_proj = inner_rows(active, d_output)
    db_proj = jnp.sum(d_output.astype(jnp.float32), axis=0)
    d_active = times_trans(d_output, back[11])
    _, gelu_pull = jax.vjp(gelu_tanh, hidden)
    d_hidden = gelu_pull(d_active)[0].astype(jnp.bfloat16)
    dw_fc = inner_rows(normed_two, d_hidden)
    db_fc = jnp.sum(d_hidden.astype(jnp.float32), axis=0)
    d_normed_two = times_trans(d_hidden, back[9])
    _, norm_pull_two = jax.vjp(
        layer_norm, resid, back[7].astype(jnp.float32), back[8].astype(jnp.float32)
    )
    d_resid_part, dg_two, db_two = norm_pull_two(d_normed_two)
    d_resid = out_grad + d_resid_part
    d_branch = d_resid.astype(jnp.bfloat16)
    dw_out = inner_rows(mixed_rows, d_branch)
    db_out = jnp.sum(d_branch.astype(jnp.float32), axis=0)
    d_mixed = times_trans(d_branch, back[5]).astype(jnp.bfloat16).reshape(seqs, span, width)

    def attend_back(item):
        q_rows, k_rows, v_rows, seq_ids, near_ids, d_rows, lse_rows = item
        length = k_rows.shape[0]
        scores = masked_scores(q_rows, k_rows, seq_ids, near_ids)
        probs = jnp.exp(scores - lse_rows[..., None])
        d_three = d_rows.reshape(span, HEADS, size)
        v_three = v_rows.reshape(length, HEADS, size)
        d_probs = jnp.einsum("qhd,khd->hqk", d_three, v_three, preferred_element_type=jnp.float32)
        delta = jnp.sum(probs * d_probs, axis=-1, keepdims=True)
        d_scores = (probs * (d_probs - delta)).astype(jnp.bfloat16)
        d_query = (
            jnp.einsum(
                "hqk,khd->qhd",
                d_scores,
                k_rows.reshape(length, HEADS, size),
                preferred_element_type=jnp.float32,
            )
            * scale
        )
        d_key = (
            jnp.einsum(
                "hqk,qhd->khd",
                d_scores,
                q_rows.reshape(span, HEADS, size),
                preferred_element_type=jnp.float32,
            )
            * scale
        )
        d_value = jnp.einsum(
            "hqk,qhd->khd", probs.astype(jnp.bfloat16), d_three, preferred_element_type=jnp.float32
        )
        return (
            d_query.reshape(span, width),
            d_key.reshape(length, width),
            d_value.reshape(length, width),
        )

    d_query, d_key_all, d_value_all = lax.map(
        attend_back, (query, keys_b, values_b, segments, segments, d_mixed, log_total)
    )
    d_key, d_value = (
        lax.psum_scatter(d_key_all, "cp", scatter_dimension=1, tiled=True),
        lax.psum_scatter(d_value_all, "cp", scatter_dimension=1, tiled=True),
    )
    d_merged = (
        jnp.concatenate([d_query, d_key, d_value], axis=-1)
        .astype(jnp.bfloat16)
        .reshape(rows, 3 * width)
    )
    d_merged_f = d_merged.astype(jnp.float32)
    db_query = jnp.sum(d_merged_f[:, :width], axis=0)
    db_value = jnp.sum(d_merged_f[:, 2 * width :], axis=0)
    dw_qkv = inner_rows(normed, d_merged)
    d_normed = times_trans(d_merged, back[2])
    _, norm_pull_one = jax.vjp(
        layer_norm, tok_rows, back[0].astype(jnp.float32), back[1].astype(jnp.float32)
    )
    d_tok_part, dg_one, db_one = norm_pull_one(d_normed)
    tokens_grad = (d_resid + d_tok_part).astype(jnp.bfloat16).reshape(seqs, span, width)
    shards = (
        lax.psum_scatter(dg_one, "fsdp", scatter_dimension=0, tiled=True),
        lax.psum_scatter(db_one, "fsdp", scatter_dimension=0, tiled=True),
        lax.psum_scatter(dw_qkv, "fsdp", scatter_dimension=0, tiled=True),
        lax.psum_scatter(db_query, "fsdp", scatter_dimension=0, tiled=True),
        lax.psum_scatter(db_value, "fsdp", scatter_dimension=0, tiled=True),
        lax.psum_scatter(dw_out, "fsdp", scatter_dimension=0, tiled=True),
        lax.psum_scatter(db_out, "fsdp", scatter_dimension=0, tiled=True),
        lax.psum_scatter(dg_two, "fsdp", scatter_dimension=0, tiled=True),
        lax.psum_scatter(db_two, "fsdp", scatter_dimension=0, tiled=True),
        lax.psum_scatter(dw_fc, "fsdp", scatter_dimension=0, tiled=True),
        lax.psum_scatter(db_fc, "fsdp", scatter_dimension=0, tiled=True),
        lax.psum_scatter(dw_proj, "fsdp", scatter_dimension=0, tiled=True),
        lax.psum_scatter(db_proj, "fsdp", scatter_dimension=0, tiled=True),
    )
    totals = lax.psum(
        (
            shards[0],
            shards[1],
            shards[2],
            shards[3],
            shards[4],
            shards[5],
            shards[6],
            shards[7],
            shards[8],
            shards[9],
            shards[10],
            shards[11],
            shards[12],
        ),
        ("cp", "rep"),
    )
    return (
        layer_out,
        tokens_grad,
        totals[0],
        totals[1],
        totals[2],
        totals[3],
        totals[4],
        totals[5],
        totals[6],
        totals[7],
        totals[8],
        totals[9],
        totals[10],
        totals[11],
        totals[12],
    )


def solution(mesh):
    placed = (
        P(("fsdp", "rep"), "cp", None),
        P(("fsdp", "rep"), None),
        P("fsdp"),
        P("fsdp"),
        P("fsdp", None),
        P("fsdp"),
        P("fsdp"),
        P("fsdp", None),
        P("fsdp"),
        P("fsdp"),
        P("fsdp"),
        P("fsdp", None),
        P("fsdp"),
        P("fsdp", None),
        P("fsdp"),
        P(("fsdp", "rep"), "cp", None),
    )
    return jax.shard_map(
        body,
        mesh=mesh,
        in_specs=placed,
        out_specs=(
            P(("fsdp", "rep"), "cp", None),
            P(("fsdp", "rep"), "cp", None),
            P("fsdp"),
            P("fsdp"),
            P("fsdp", None),
            P("fsdp"),
            P("fsdp"),
            P("fsdp", None),
            P("fsdp"),
            P("fsdp"),
            P("fsdp"),
            P("fsdp", None),
            P("fsdp"),
            P("fsdp", None),
            P("fsdp"),
        ),
        check_vma=False,
    )
```

profile of v0, /device:TPU:0, one launch (start us, length us, event | category | flops | bytes accessed | tf_op | source)
XLA Modules:
  0.0 1499.2 jit_solution(1097224443274911993)
XLA Ops:
  50.4 56.1 %all-gather.20.cloned.1.call-done = bf16[2,2048,768]{1,2,0:T(8,128)(2,1)} async-done(((bf16[2,512,768]{1,2,0:T(8,128)(2,1)}), bf16[2,2048,768]{1,2,0:T(8,128)(2,1)}) %all-gather.20.cloned.1.call-update) | async-done | bytes 6291472 | tf_op jit(solution)/shard_map/all_gather | solution.py:89
  106.5 72.5 %all-gather.18.cloned.1.call-done = bf16[2,2048,768]{1,2,0:T(8,128)(2,1)} async-done(((bf16[2,512,768]{1,2,0:T(8,128)(2,1)}), bf16[2,2048,768]{1,2,0:T(8,128)(2,1)}) %all-gather.18.cloned.1.call-update) | async-done | bytes 6291472 | tf_op jit(solution)/shard_map/all_gather | solution.py:90
  178.9 155.2 %while.34 = (s32[]{:T(128)}, bf16[2,512,768]{2,1,0:T(8,128)(2,1)}, f32[2,12,512]{2,1,0:T(8,128)S(1)}, bf16[2,2048,768]{1,2,0:T(8,128)(2,1)}, s32[2,2048]{1,0:T(2...) while((s32[]{:T(128)}, bf16[2,512,768]{2,1,0:T(8,128)(2,1)}, ...), condition=%wide.region_5.6_spmd.clone, body=%wide.region_2.5_spmd.clone.sunk | while | flops 3375753728 | bytes 197388496 | solution.py:127
  188.6 23.9 %fusion.106 = (f32[12,512]{1,0:T(8,128)S(1)}, f32[12,512,2048]{2,1,0:T(8,128)}) fusion(pred[512,2048]{1,0:T(8,128)(4,1)} %fusion.105, bf16[512,12,64]{0,2,1:T(8,128)(2,1)} %bitcast.170, bf16[2048,12,64]{0,2,1:T(8,128)(2,1)S(1)} %bitcast.165), kind=kOutput, calls=%fused_computation.5.clone.1 | convolution fusion | flops 1648355328 | bytes 55336960 | tf_op jit(solution)/shard_map/while/body/eval_jaxpr/qhd,khd->hqk/dot_general | solution.py:99
  212.5 24.5 %fusion.107 = f32[12,512]{1,0:T(8,128)S(1)} fusion(f32[12,512,2048]{2,1,0:T(8,128)} %get-tuple-element.683, f32[12,512]{1,0:T(8,128)S(1)} %get-tuple-element.684, pred[512,2048]{1,0:T(8,128)(4,1)} %fusion.105), kind=kLoop, calls=%fused_computation.6.clone.1 | loop fusion | flops 50325504 | bytes 51429376 | tf_op jit(solution)/shard_map/while/body/eval_jaxpr/reduce_sum | solution.py:114
  237.1 20.2 %fusion.108 = bf16[12,64,512]{2,1,0:T(8,128)(2,1)S(1)} fusion(bf16[2048,12,64]{0,2,1:T(8,128)(2,1)S(1)} %bitcast.174, f32[12,512,2048]{2,1,0:T(8,128)} %get-tuple-element.683, f32[12,512]{1,0:T(8,128)S(1)} %fusion.107, f32[12,512]{1,0:T(8,128)S(1)} %get-tuple-element.684, pred[512,2048]{1,0:T(8,128)(4,1)S(1)} %copy-done), kind=kOutput, calls=%fused_computation.10.clone.1 | convolution fusion | flops 1673920512 | bytes 55361536 | tf_op jit(solution)/shard_map/while/body/eval_jaxpr/hqk,khd->qhd/dot_general | solution.py:116
  268.2 21.5 %fusion.106 = (f32[12,512]{1,0:T(8,128)S(1)}, f32[12,512,2048]{2,1,0:T(8,128)}) fusion(pred[512,2048]{1,0:T(8,128)(4,1)} %fusion.105, bf16[512,12,64]{0,2,1:T(8,128)(2,1)} %bitcast.170, bf16[2048,12,64]{0,2,1:T(8,128)(2,1)S(1)} %bitcast.165), kind=kOutput, calls=%fused_computation.5.clone.1 | convolution fusion | flops 1648355328 | bytes 55336960 | tf_op jit(solution)/shard_map/while/body/eval_jaxpr/qhd,khd->hqk/dot_general | solution.py:99
  289.7 22.9 %fusion.107 = f32[12,512]{1,0:T(8,128)S(1)} fusion(f32[12,512,2048]{2,1,0:T(8,128)} %get-tuple-element.683, f32[12,512]{1,0:T(8,128)S(1)} %get-tuple-element.684, pred[512,2048]{1,0:T(8,128)(4,1)} %fusion.105), kind=kLoop, calls=%fused_computation.6.clone.1 | loop fusion | flops 50325504 | bytes 51429376 | tf_op jit(solution)/shard_map/while/body/eval_jaxpr/reduce_sum | solution.py:114
  312.5 20.2 %fusion.108 = bf16[12,64,512]{2,1,0:T(8,128)(2,1)S(1)} fusion(bf16[2048,12,64]{0,2,1:T(8,128)(2,1)S(1)} %bitcast.174, f32[12,512,2048]{2,1,0:T(8,128)} %get-tuple-element.683, f32[12,512]{1,0:T(8,128)S(1)} %fusion.107, f32[12,512]{1,0:T(8,128)S(1)} %get-tuple-element.684, pred[512,2048]{1,0:T(8,128)(4,1)S(1)} %copy-done), kind=kOutput, calls=%fused_computation.10.clone.1 | convolution fusion | flops 1673920512 | bytes 55361536 | tf_op jit(solution)/shard_map/while/body/eval_jaxpr/hqk,khd->qhd/dot_general | solution.py:116
  379.7 375.4 %while.35 = (s32[]{:T(128)}, bf16[2,512,768]{2,1,0:T(8,128)(2,1)}, f32[2,2048,768]{2,1,0:T(8,128)}, f32[2,2048,768]{2,1,0:T(8,128)}, bf16[2,2048,768]{1,2,0:T(8,...) while((s32[]{:T(128)}, bf16[2,512,768]{2,1,0:T(8,128)(2,1)}, ...), condition=%wide.region_12.13_spmd.clone, body=%wide.region_10.12_spmd.clone.sunk | while | flops 8247306752 | bytes 519514368 | solution.py:218
  392.5 20.5 %fusion.119 = f32[12,512,2048]{2,1,0:T(8,128)} fusion(bf16[512,12,64]{0,2,1:T(8,128)(2,1)} %bitcast.167, bf16[2048,12,64]{0,2,1:T(8,128)(2,1)S(1)} %bitcast.162), kind=kOutput, calls=%fused_computation.114.clone.1 | convolution fusion | flops 1610612736 | bytes 54263808 | tf_op jit(solution)/shard_map/while/body/eval_jaxpr/qhd,khd->hqk/dot_general | solution.py:99
  413.0 23.1 %fusion.121 = f32[12,64,2048]{2,1,0:T(8,128)} fusion(bf16[512,12,64]{0,2,1:T(8,128)(2,1)} %bitcast.172, f32[12,512,2048]{2,1,0:T(8,128)} %fusion.119, f32[12,512]{1,0:T(8,128)S(1)} %dynamic-slice_bitcast_fusion.2, pred[512,2048]{1,0:T(8,128)(4,1)} %fusion.120), kind=kOutput, calls=%fused_computation.24.clone.1 | convolution fusion | flops 1660944384 | bytes 58482688 | tf_op jit(solution)/shard_map/while/body/eval_jaxpr/hqk,qhd->khd/dot_general | solution.py:209
  442.7 37.6 %multiply_reduce_fusion.5 = (f32[12,512]{1,0:T(8,128)S(1)}, f32[12,512,2048]{2,1,0:T(8,128)}) fusion(f32[12,512,2048]{2,1,0:T(8,128)} %fusion.119, f32[12,512]{1,0:T(8,128)S(1)} %dynamic-slice_bitcast_fusion.2, pred[512,2048]{1,0:T(8,128)(4,1)} %fusion.120, bf16[512,12,64]{0,2,1:T(8,128)(2,1)} %bitcast.173, bf16[2048,12,64]{0,2,1:T(8,128)(2,1)} %bitcast.166), kind=kOutput, calls=%fused_computation.21.clone.1 | convolution fusion | flops 1673521152 | bytes 105693184 | tf_op jit(solution)/shard_map/while/body/eval_jaxpr/qhd,khd->hqk/dot_general | solution.py:188
  480.3 41.4 %multiply_convert_fusion.5 = bf16[12,512,2048]{2,1,0:T(8,128)(2,1)} fusion(f32[12,512,2048]{2,1,0:T(8,128)} %get-tuple-element.697, f32[12,512,2048]{2,1,0:T(8,128)} %fusion.119, f32[12,512]{1,0:T(8,128)S(1)} %get-tuple-element.698, f32[12,512]{1,0:T(8,128)S(1)} %dynamic-slice_bitcast_fusion.2, pred[512,2048]{1,0:T(8,128)(4,1)} %fusion.120), kind=kLoop, calls=%fused_computation.20.clone.1 | loop fusion | flops 75497472 | bytes 126926848 | tf_op jit(solution)/shard_map/while/body/eval_jaxpr/convert_element_type | solution.py:190
  578.6 20.5 %fusion.119 = f32[12,512,2048]{2,1,0:T(8,128)} fusion(bf16[512,12,64]{0,2,1:T(8,128)(2,1)} %bitcast.167, bf16[2048,12,64]{0,2,1:T(8,128)(2,1)S(1)} %bitcast.162), kind=kOutput, calls=%fused_computation.114.clone.1 | convolution fusion | flops 1610612736 | bytes 54263808 | tf_op jit(solution)/shard_map/while/body/eval_jaxpr/qhd,khd->hqk/dot_general | solution.py:99
  599.1 23.1 %fusion.121 = f32[12,64,2048]{2,1,0:T(8,128)} fusion(bf16[512,12,64]{0,2,1:T(8,128)(2,1)} %bitcast.172, f32[12,512,2048]{2,1,0:T(8,128)} %fusion.119, f32[12,512]{1,0:T(8,128)S(1)} %dynamic-slice_bitcast_fusion.2, pred[512,2048]{1,0:T(8,128)(4,1)} %fusion.120), kind=kOutput, calls=%fused_computation.24.clone.1 | convolution fusion | flops 1660944384 | bytes 58482688 | tf_op jit(solution)/shard_map/while/body/eval_jaxpr/hqk,qhd->khd/dot_general | solution.py:209
  628.9 37.6 %multiply_reduce_fusion.5 = (f32[12,512]{1,0:T(8,128)S(1)}, f32[12,512,2048]{2,1,0:T(8,128)}) fusion(f32[12,512,2048]{2,1,0:T(8,128)} %fusion.119, f32[12,512]{1,0:T(8,128)S(1)} %dynamic-slice_bitcast_fusion.2, pred[512,2048]{1,0:T(8,128)(4,1)} %fusion.120, bf16[512,12,64]{0,2,1:T(8,128)(2,1)} %bitcast.173, bf16[2048,12,64]{0,2,1:T(8,128)(2,1)} %bitcast.166), kind=kOutput, calls=%fused_computation.21.clone.1 | convolution fusion | flops 1673521152 | bytes 105693184 | tf_op jit(solution)/shard_map/while/body/eval_jaxpr/qhd,khd->hqk/dot_general | solution.py:188
  666.4 41.4 %multiply_convert_fusion.5 = bf16[12,512,2048]{2,1,0:T(8,128)(2,1)} fusion(f32[12,512,2048]{2,1,0:T(8,128)} %get-tuple-element.697, f32[12,512,2048]{2,1,0:T(8,128)} %fusion.119, f32[12,512]{1,0:T(8,128)S(1)} %get-tuple-element.698, f32[12,512]{1,0:T(8,128)S(1)} %dynamic-slice_bitcast_fusion.2, pred[512,2048]{1,0:T(8,128)(4,1)} %fusion.120), kind=kLoop, calls=%fused_computation.20.clone.1 | loop fusion | flops 75497472 | bytes 126926848 | tf_op jit(solution)/shard_map/while/body/eval_jaxpr/convert_element_type | solution.py:190
  787.2 88.8 %reduce-scatter.9.cloned.1.call-done = f32[2,512,768]{2,1,0:T(8,128)} async-done(((f32[2,2048,768]{2,1,0:T(8,128)}), f32[2,512,768]{2,1,0:T(8,128)}) %reduce-scatter.9.cloned.1.call-update) | async-done | bytes 3145744 | tf_op jit(solution)/shard_map/reduce_scatter | solution.py:223
  878.1 121.8 %reduce-scatter.7.cloned.1.call-done = f32[2,512,768]{2,1,0:T(8,128)} async-done(((f32[2,2048,768]{2,1,0:T(8,128)}), f32[2,512,768]{2,1,0:T(8,128)}) %reduce-scatter.7.cloned.1.call-update) | async-done | bytes 3145744 | tf_op jit(solution)/shard_map/reduce_scatter | solution.py:222
  1012.7 21.2 %reduce-scatter.15.cloned.1.call-done = f32[384,3072]{1,0:T(8,128)} async-done(((f32[768,3072]{1,0:T(8,128)}), f32[384,3072]{1,0:T(8,128)}) %reduce-scatter.15.cloned.1.call-update) | async-done | bytes 4718608 | tf_op jit(solution)/shard_map/reduce_scatter | solution.py:250
  1033.9 21.5 %reduce-scatter.17.cloned.1.call-done = f32[1536,768]{1,0:T(8,128)} async-done(((f32[3072,768]{1,0:T(8,128)}), f32[1536,768]{1,0:T(8,128)}) %reduce-scatter.17.cloned.1.call-update) | async-done | bytes 4718608 | tf_op jit(solution)/shard_map/reduce_scatter | solution.py:252
  1108.0 82.4 %all-reduce.9 = (f32[384]{0:T(512)}, f32[384]{0:T(512)}, f32[384]{0:T(512)}, f32[384]{0:T(512)}, f32[384]{0:T(512)}, /*index=5*/f32[384]{0:T(512)}, f32[384]{0:T(512)}, f32[1536]{0:T(1024)}, f32[384]{0:T(512)}) all-reduce(f32[384]{0:T(512)S(1)} %dynamic-slice.11, ...), channel_id=1, replica_groups=mesh['cp'=4,'fsdp'=2,'rep'=4] {'cp','rep'}, use_global_device_ids=true, to_apply=%region_19.20 | all-reduce | flops 4608 | bytes 36864 | tf_op jit(solution)/shard_map/psum | solution.py:255
  1195.0 286.7 %all-reduce.14.cloned.1.call-done = (f32[384,2304]{1,0:T(8,128)}, f32[384,768]{1,0:T(8,128)}, f32[384,3072]{1,0:T(8,128)}, f32[1536,768]{1,0:T(8,128)}) async-done(((f32[384,2304]{1,0:T(8,128)}, f32[384,768]{1,0:T(8,128)}, f32[384,3072]{1,0:T(8,128)}, f32[1536,768]{1,0:T(8,128)}), (f32[384,2304]{1,0:T(8,128)}, f32[384,768]{1,0:T(8,128)}, f32[384,3072]{1,0:T(8,128)}, ...) | async-done | bytes 14155792 | tf_op jit(solution)/shard_map/psum | solution.py:255
  (319 shorter events, 350.1 us)
Async XLA Ops:
  7.2 17.8 %all-gather.16.cloned.1.call-start = ((), (), s32[]{:S(2)}) async-start(), calls=%async_computation.6 | async-start | bytes 5308416 | tf_op jit(solution)/shard_map/all_gather | solution.py:62
  7.9 98.5 %all-gather.20.cloned.1.call-start = ((), (), s32[]{:S(2)}) async-start(), calls=%async_computation.8 | async-start | bytes 7864320 | tf_op jit(solution)/shard_map/all_gather | solution.py:89
  35.1 143.8 %all-gather.18.cloned.1.call-start = ((), (), s32[]{:S(2)}) async-start(), calls=%async_computation.7 | async-start | bytes 7864320 | tf_op jit(solution)/shard_map/all_gather | solution.py:90
  36.8 297.3 %all-gather.22.cloned.1.call-start = ((), (), s32[]{:S(2)}) async-start(), calls=%async_computation.9 | async-start | bytes 1769472 | tf_op jit(solution)/shard_map/all_gather | solution.py:65
  37.4 141.6 %copy-start.23 = (s32[2,2048]{1,0:T(2,128)S(1)}, s32[2,2048]{1,0:T(2,128)}, u32[]{:S(2)}) copy-start(s32[2,2048]{1,0:T(2,128)} %param.21) | copy-start | bytes 49156
  37.4 301.1 %all-gather.24.cloned.1.call-start = ((), (), s32[]{:S(2)}) async-start(), calls=%async_computation.10 | async-start | bytes 7077888 | tf_op jit(solution)/shard_map/all_gather | solution.py:69
  38.0 311.6 %all-gather.26.cloned.1.call-start = ((), (), s32[]{:S(2)}) async-start(), calls=%async_computation.11 | async-start | bytes 7077888 | tf_op jit(solution)/shard_map/all_gather | solution.py:71
  38.5 837.5 %reduce-scatter.9.cloned.1.call-start = ((), (), s32[]{:S(2)}) async-start(), calls=%async_computation.13 | async-start | bytes 15728640 | tf_op jit(solution)/shard_map/reduce_scatter | solution.py:223
  178.9 155.2 %copy-start.46 = (f32[768]{0:T(1024)S(1)}, f32[768]{0:T(1024)}, u32[]{:S(2)}) copy-start(f32[768]{0:T(1024)} %reshape.447) | copy-start | bytes 9220
  212.5 24.5 %copy-start = (pred[512,2048]{1,0:T(8,128)(4,1)S(1)}, pred[512,2048]{1,0:T(8,128)(4,1)}, u32[]{:S(2)}) copy-start(pred[512,2048]{1,0:T(8,128)(4,1)} %fusion.105) | copy-start | bytes 3145732 | tf_op jit(solution)/shard_map/while
  212.5 24.5 %copy-start.3 = (bf16[1,2048,768]{1,2,0:T(8,128)(2,1)S(1)}, bf16[1,2048,768]{1,2,0:T(8,128)(2,1)}, u32[]{:S(2)}) copy-start(bf16[1,2048,768]{1,2,0:T(8,128)(2,1)} %get-tuple-element.681) | copy-start | bytes 9437188 | tf_op jit(solution)/shard_map/while
  289.6 22.9 %copy-start = (pred[512,2048]{1,0:T(8,128)(4,1)S(1)}, pred[512,2048]{1,0:T(8,128)(4,1)}, u32[]{:S(2)}) copy-start(pred[512,2048]{1,0:T(8,128)(4,1)} %fusion.105) | copy-start | bytes 3145732 | tf_op jit(solution)/shard_map/while
  289.6 22.9 %copy-start.3 = (bf16[1,2048,768]{1,2,0:T(8,128)(2,1)S(1)}, bf16[1,2048,768]{1,2,0:T(8,128)(2,1)}, u32[]{:S(2)}) copy-start(bf16[1,2048,768]{1,2,0:T(8,128)(2,1)} %get-tuple-element.681) | copy-start | bytes 9437188 | tf_op jit(solution)/shard_map/while
  337.9 36.6 %copy-start.6 = (f32[1024,768]{1,0:T(8,128)}, f32[1024,768]{1,0:T(8,128)S(1)}, u32[]{:S(2)}) copy-start(f32[1024,768]{1,0:T(8,128)S(1)} %get-tuple-element.552) | copy-start | bytes 9437188
  338.0 36.6 %copy-start.24 = (f32[1024]{0:T(1024)}, f32[1024]{0:T(1024)S(1)}, u32[]{:S(2)}) copy-start(f32[1024]{0:T(1024)S(1)} %broadcast_multiply_fusion) | copy-start | bytes 12292
  338.5 36.1 %copy-start.26 = (f32[1024]{0:T(1024)}, f32[1024]{0:T(1024)S(1)}, u32[]{:S(2)}) copy-start(f32[1024]{0:T(1024)S(1)} %fusion.36) | copy-start | bytes 12292
  755.1 244.8 %reduce-scatter.7.cloned.1.call-start = ((), (), s32[]{:S(2)}) async-start(), calls=%async_computation.12 | async-start | bytes 15728640 | tf_op jit(solution)/shard_map/reduce_scatter | solution.py:222
  755.9 256.8 %reduce-scatter.13.cloned.1.call-start = ((), (), s32[]{:S(2)}) async-start(), calls=%async_computation.15 | async-start | bytes 3538944 | tf_op jit(solution)/shard_map/reduce_scatter | solution.py:246
  760.9 273.0 %reduce-scatter.15.cloned.1.call-start = ((), (), s32[]{:S(2)}) async-start(), calls=%async_computation.16 | async-start | bytes 14155776 | tf_op jit(solution)/shard_map/reduce_scatter | solution.py:250
  772.6 282.7 %reduce-scatter.17.cloned.1.call-start = ((), (), s32[]{:S(2)}) async-start(), calls=%async_computation.17 | async-start | bytes 14155776 | tf_op jit(solution)/shard_map/reduce_scatter | solution.py:252
  787.0 287.5 %reduce-scatter.11.cloned.1.call-start = ((), (), s32[]{:S(2)}) async-start(), calls=%async_computation.14 | async-start | bytes 10616832 | tf_op jit(solution)/shard_map/reduce_scatter | solution.py:243
  878.1 133.4 %copy-start.15 = (bf16[2,512,768]{2,1,0:T(8,128)(2,1)}, bf16[2,512,768]{2,1,0:T(8,128)(2,1)S(1)}, u32[]{:S(2)}) copy-start(bf16[2,512,768]{2,1,0:T(8,128)(2,1)S(1)} %convert.15) | copy-start | bytes 4718596
  1011.5 470.1 %all-reduce.14.cloned.1.call-start = ((), (), s32[]{:S(2)}) async-start(), calls=%async_computation.18 | async-start | bytes 28311552 | tf_op jit(solution)/shard_map/psum | solution.py:255
  1101.7 88.7 %copy-start.39 = (f32[1024]{0:T(1024)S(1)}, f32[1024]{0:T(1024)}, u32[]{:S(2)}) copy-start(f32[1024]{0:T(1024)} %copy-done.38) | copy-start | bytes 12292
  (57 other events, 347.4 us)
Sparse Core Ops, SparseCore 0:
  9.6 15.3 all-gather.15
  35.2 71.1 all-gather.19
  108.9 70.0 all-gather.17
  180.3 9.2 all-gather.21
  191.0 15.5 all-gather.23
  208.0 15.6 all-gather.25
  755.2 120.7 reduce-scatter.8
  879.2 120.7 reduce-scatter.6
  1002.8 9.8 reduce-scatter.12
  1014.9 18.9 reduce-scatter.14
  1036.3 19.0 reduce-scatter.16
  1057.7 16.8 reduce-scatter.10
  1081.0 400.6 all-reduce.13
where the time goes:
time: 1500 us
  waiting for transfers between devices  695 us (46%)
  matrix products  410 us (27%)
  other arithmetic  160 us (11%)
  local copies, waits for them, and re-layouts  111 us (7%)
  blocking collectives  103 us (7%)
  between operations  16.3 us (1%)
    psum x1, waiting for transfers between devices, body(): lax.psum((shards[0], shards[1], shards[2], shards[3], shards[4], shards[5...  287 us
    reduce_scatter x1, waiting for transfers between devices, body(): lax.psum_scatter(d_key_all, 'cp', scatter_dimension=1, tiled=True)  122 us
    reduce_scatter x1, waiting for transfers between devices, body(): lax.psum_scatter(d_value_all, 'cp', scatter_dimension=1, tiled=True)  88.8 us
    dot_general x4, matrix products, masked_scores(): jnp.einsum('qhd,khd->hqk', q_three, k_three, preferred_element_type=jnp.f...  86.3 us
    convert_element_type x2, other arithmetic, attend_back(): d_scores = (probs * (d_probs - delta)).astype(jnp.bfloat16)  82.8 us
    psum x1, blocking collectives, body(): lax.psum((shards[0], shards[1], shards[2], shards[3], shards[4], shards[5...  82.4 us
    dot_general x2, matrix products, attend_back(): jnp.einsum('qhd,khd->hqk', d_three, v_three, preferred_element_type=jnp.f...  75.1 us
    all_gather x1, waiting for transfers between devices, body(): lax.all_gather(value_loc, 'cp', axis=1, tiled=True)  72.5 us
  transfers between devices with their start and end apart: 13, of which 10 were waited for; matrix products, arithmetic and copies ran while one was open for 17% of the time, Pallas kernels for 0%

commit v1 on v0

--- a/solution.py
+++ b/solution.py
@@ -4,6 +4,11 @@
 from jax.sharding import PartitionSpec as P
 
 HEADS = 12
+
+
+def gather_over(x, axis, d):
+    sent = jnp.stack([x] * lax.axis_size(axis))
+    return jnp.concatenate(lax.all_to_all(sent, axis, 0, 0), axis=d)
 
 
 def layer_norm(value, gain, shift):
@@ -86,7 +91,7 @@
     key_loc = merged[:, :, width : 2 * width]
     value_loc = merged[:, :, 2 * width :]
     keys_all, values_all = (
-        lax.all_gather(key_loc, "cp", axis=1, tiled=True),
+        gather_over(key_loc, "cp", 1),
         lax.all_gather(value_loc, "cp", axis=1, tiled=True),
     )
     key_pos = jnp.arange(seq_len)

time: 1500 us -> 1510 us (level)
  waiting for transfers between devices: 695 us -> 666 us
  local copies, waits for them, and re-layouts: 111 us -> 135 us
    all_to_all x0 -> x1, waiting for transfers between devices: none -> 86.2 us  [gather_over(): return jnp.concatenate(lax.all_to_all(sent, axis, 0, 0), axis=d)]
    all_gather x1, waiting for transfers between devices: 72.5 us -> 12.3 us  [body(): lax.all_gather(value_loc, 'cp', axis=1, tiled=True)]
    all_gather x1, waiting for transfers between devices: 56.1 us -> 0.02 us  [body(): lax.all_gather(key_loc, 'cp', axis=1, tiled=True)]
    dynamic_slice x18 -> x22, local copies, waits for them, and re-layouts: 30 us -> 41.3 us  [body(): lax.map(attend, (query, keys_all, values_all, segments, segments))]
  transfers between devices with their start and end apart: 13 -> 14, of which waited for: 10 -> 10; matrix products, arithmetic and copies ran while one was open for 17% -> 20% of each run, Pallas kernels for 0% -> 0%
where the time goes in v1:
time: 1510 us; the launch traced here: 1500 us
  waiting for transfers between devices  666 us (44%)
  matrix products  411 us (27%)
  other arithmetic  159 us (11%)
  local copies, waits for them, and re-layouts  135 us (9%)
  blocking collectives  102 us (7%)
  between operations  16.3 us (1%)
    psum x1, waiting for transfers between devices, body(): lax.psum((shards[0], shards[1], shards[2], shards[3], shards[4], shards[5...  287 us
    reduce_scatter x1, waiting for transfers between devices, body(): lax.psum_scatter(d_key_all, 'cp', scatter_dimension=1, tiled=True)  122 us
    reduce_scatter x1, waiting for transfers between devices, body(): lax.psum_scatter(d_value_all, 'cp', scatter_dimension=1, tiled=True)  89.2 us
    dot_general x4, matrix products, masked_scores(): jnp.einsum('qhd,khd->hqk', q_three, k_three, preferred_element_type=jnp.f...  86.9 us
    all_to_all x1, waiting for transfers between devices, gather_over(): return jnp.concatenate(lax.all_to_all(sent, axis, 0, 0), axis=d)  86.2 us
    convert_element_type x2, other arithmetic, attend_back(): d_scores = (probs * (d_probs - delta)).astype(jnp.bfloat16)  82.9 us
    psum x1, blocking collectives, body(): lax.psum((shards[0], shards[1], shards[2], shards[3], shards[4], shards[5...  82.5 us
    dot_general x2, matrix products, attend_back(): jnp.einsum('qhd,khd->hqk', d_three, v_three, preferred_element_type=jnp.f...  75.2 us
  transfers between devices with their start and end apart: 14, of which 10 were waited for; matrix products, arithmetic and copies ran while one was open for 20% of the time, Pallas kernels for 0%

profile of v1, /device:TPU:0, one launch (start us, length us, event | category | flops | bytes accessed | tf_op | source)
XLA Modules:
  0.0 1498.2 jit_solution(17773981939482871922)
XLA Ops:
  58.1 86.2 %all-to-all-done = bf16[4,2,512,768]{2,3,1,0:T(8,128)(2,1)} async-done(((bf16[4,2,512,768]{2,3,1,0:T(8,128)(2,1)}), bf16[4,2,512,768]{2,3,1,0:T(8,128)(2,1)}, u32[]{:S(2)}, u32[]{:S(2)}) %all-to-all-start) | async-done | bytes 6291488 | tf_op jit(solution)/shard_map/all_to_all | solution.py:11
  165.3 166.8 %while.34 = (s32[]{:T(128)}, bf16[2,512,768]{2,1,0:T(8,128)(2,1)}, f32[2,12,512]{2,1,0:T(8,128)S(1)}, bf16[2,2048,768]{1,2,0:T(8,128)(2,1)}, s32[2,2048]{1,0:T(2...) while((s32[]{:T(128)}, bf16[2,512,768]{2,1,0:T(8,128)(2,1)}, ...), condition=%wide.region_5.6_spmd.clone, body=%wide.region_2.5_spmd.clone.sunk | while | flops 3375753728 | bytes 203679984 | solution.py:132
  181.1 24.5 %fusion.106 = (f32[12,512]{1,0:T(8,128)S(1)}, f32[12,512,2048]{2,1,0:T(8,128)}) fusion(pred[512,2048]{1,0:T(8,128)(4,1)} %fusion.105, bf16[512,12,64]{0,2,1:T(8,128)(2,1)} %bitcast.173, bf16[2048,12,64]{0,2,1:T(8,128)(2,1)S(1)} %bitcast.168), kind=kOutput, calls=%fused_computation.5.clone.1 | convolution fusion | flops 1648355328 | bytes 55336960 | tf_op jit(solution)/shard_map/while/body/eval_jaxpr/qhd,khd->hqk/dot_general | solution.py:104
  205.6 23.9 %fusion.107 = f32[12,512]{1,0:T(8,128)S(1)} fusion(f32[12,512,2048]{2,1,0:T(8,128)} %get-tuple-element.698, f32[12,512]{1,0:T(8,128)S(1)} %get-tuple-element.699, pred[512,2048]{1,0:T(8,128)(4,1)} %fusion.105), kind=kLoop, calls=%fused_computation.6.clone.1 | loop fusion | flops 50325504 | bytes 51429376 | tf_op jit(solution)/shard_map/while/body/eval_jaxpr/reduce_sum | solution.py:119
  229.5 20.2 %fusion.108 = bf16[12,64,512]{2,1,0:T(8,128)(2,1)S(1)} fusion(bf16[2048,12,64]{0,2,1:T(8,128)(2,1)S(1)} %bitcast.177, f32[12,512,2048]{2,1,0:T(8,128)} %get-tuple-element.698, f32[12,512]{1,0:T(8,128)S(1)} %fusion.107, f32[12,512]{1,0:T(8,128)S(1)} %get-tuple-element.699, pred[512,2048]{1,0:T(8,128)(4,1)S(1)} %copy-done), kind=kOutput, calls=%fused_computation.10.clone.1 | convolution fusion | flops 1673920512 | bytes 55361536 | tf_op jit(solution)/shard_map/while/body/eval_jaxpr/hqk,khd->qhd/dot_general | solution.py:121
  266.2 21.5 %fusion.106 = (f32[12,512]{1,0:T(8,128)S(1)}, f32[12,512,2048]{2,1,0:T(8,128)}) fusion(pred[512,2048]{1,0:T(8,128)(4,1)} %fusion.105, bf16[512,12,64]{0,2,1:T(8,128)(2,1)} %bitcast.173, bf16[2048,12,64]{0,2,1:T(8,128)(2,1)S(1)} %bitcast.168), kind=kOutput, calls=%fused_computation.5.clone.1 | convolution fusion | flops 1648355328 | bytes 55336960 | tf_op jit(solution)/shard_map/while/body/eval_jaxpr/qhd,khd->hqk/dot_general | solution.py:104
  287.7 22.8 %fusion.107 = f32[12,512]{1,0:T(8,128)S(1)} fusion(f32[12,512,2048]{2,1,0:T(8,128)} %get-tuple-element.698, f32[12,512]{1,0:T(8,128)S(1)} %get-tuple-element.699, pred[512,2048]{1,0:T(8,128)(4,1)} %fusion.105), kind=kLoop, calls=%fused_computation.6.clone.1 | loop fusion | flops 50325504 | bytes 51429376 | tf_op jit(solution)/shard_map/while/body/eval_jaxpr/reduce_sum | solution.py:119
  310.5 20.2 %fusion.108 = bf16[12,64,512]{2,1,0:T(8,128)(2,1)S(1)} fusion(bf16[2048,12,64]{0,2,1:T(8,128)(2,1)S(1)} %bitcast.177, f32[12,512,2048]{2,1,0:T(8,128)} %get-tuple-element.698, f32[12,512]{1,0:T(8,128)S(1)} %fusion.107, f32[12,512]{1,0:T(8,128)S(1)} %get-tuple-element.699, pred[512,2048]{1,0:T(8,128)(4,1)S(1)} %copy-done), kind=kOutput, calls=%fused_computation.10.clone.1 | convolution fusion | flops 1673920512 | bytes 55361536 | tf_op jit(solution)/shard_map/while/body/eval_jaxpr/hqk,khd->qhd/dot_general | solution.py:121
  379.4 373.9 %while.35 = (s32[]{:T(128)}, bf16[2,512,768]{2,1,0:T(8,128)(2,1)}, f32[2,2048,768]{2,1,0:T(8,128)}, f32[2,2048,768]{2,1,0:T(8,128)}, bf16[2,2048,768]{1,2,0:T(8,...) while((s32[]{:T(128)}, bf16[2,512,768]{2,1,0:T(8,128)(2,1)}, ...), condition=%wide.region_12.13_spmd.clone, body=%wide.region_10.12_spmd.clone.sunk | while | flops 8247306752 | bytes 519514368 | solution.py:223
  390.5 20.5 %fusion.119 = f32[12,512,2048]{2,1,0:T(8,128)} fusion(bf16[512,12,64]{0,2,1:T(8,128)(2,1)} %bitcast.170, bf16[2048,12,64]{0,2,1:T(8,128)(2,1)S(1)} %bitcast.165), kind=kOutput, calls=%fused_computation.114.clone.1 | convolution fusion | flops 1610612736 | bytes 54263808 | tf_op jit(solution)/shard_map/while/body/eval_jaxpr/qhd,khd->hqk/dot_general | solution.py:104
  411.0 23.1 %fusion.121 = f32[12,64,2048]{2,1,0:T(8,128)} fusion(bf16[512,12,64]{0,2,1:T(8,128)(2,1)} %bitcast.175, f32[12,512,2048]{2,1,0:T(8,128)} %fusion.119, f32[12,512]{1,0:T(8,128)S(1)} %dynamic-slice_bitcast_fusion.2, pred[512,2048]{1,0:T(8,128)(4,1)} %fusion.120), kind=kOutput, calls=%fused_computation.24.clone.1 | convolution fusion | flops 1660944384 | bytes 58482688 | tf_op jit(solution)/shard_map/while/body/eval_jaxpr/hqk,qhd->khd/dot_general | solution.py:214
  440.8 37.6 %multiply_reduce_fusion.5 = (f32[12,512]{1,0:T(8,128)S(1)}, f32[12,512,2048]{2,1,0:T(8,128)}) fusion(f32[12,512,2048]{2,1,0:T(8,128)} %fusion.119, f32[12,512]{1,0:T(8,128)S(1)} %dynamic-slice_bitcast_fusion.2, pred[512,2048]{1,0:T(8,128)(4,1)} %fusion.120, bf16[512,12,64]{0,2,1:T(8,128)(2,1)} %bitcast.176, bf16[2048,12,64]{0,2,1:T(8,128)(2,1)} %bitcast.169), kind=kOutput, calls=%fused_computation.21.clone.1 | convolution fusion | flops 1673521152 | bytes 105693184 | tf_op jit(solution)/shard_map/while/body/eval_jaxpr/qhd,khd->hqk/dot_general | solution.py:193
  478.4 41.4 %multiply_convert_fusion.5 = bf16[12,512,2048]{2,1,0:T(8,128)(2,1)} fusion(f32[12,512,2048]{2,1,0:T(8,128)} %get-tuple-element.712, f32[12,512,2048]{2,1,0:T(8,128)} %fusion.119, f32[12,512]{1,0:T(8,128)S(1)} %get-tuple-element.713, f32[12,512]{1,0:T(8,128)S(1)} %dynamic-slice_bitcast_fusion.2, pred[512,2048]{1,0:T(8,128)(4,1)} %fusion.120), kind=kLoop, calls=%fused_computation.20.clone.1 | loop fusion | flops 75497472 | bytes 126926848 | tf_op jit(solution)/shard_map/while/body/eval_jaxpr/convert_element_type | solution.py:195
  576.8 20.5 %fusion.119 = f32[12,512,2048]{2,1,0:T(8,128)} fusion(bf16[512,12,64]{0,2,1:T(8,128)(2,1)} %bitcast.170, bf16[2048,12,64]{0,2,1:T(8,128)(2,1)S(1)} %bitcast.165), kind=kOutput, calls=%fused_computation.114.clone.1 | convolution fusion | flops 1610612736 | bytes 54263808 | tf_op jit(solution)/shard_map/while/body/eval_jaxpr/qhd,khd->hqk/dot_general | solution.py:104
  597.2 23.1 %fusion.121 = f32[12,64,2048]{2,1,0:T(8,128)} fusion(bf16[512,12,64]{0,2,1:T(8,128)(2,1)} %bitcast.175, f32[12,512,2048]{2,1,0:T(8,128)} %fusion.119, f32[12,512]{1,0:T(8,128)S(1)} %dynamic-slice_bitcast_fusion.2, pred[512,2048]{1,0:T(8,128)(4,1)} %fusion.120), kind=kOutput, calls=%fused_computation.24.clone.1 | convolution fusion | flops 1660944384 | bytes 58482688 | tf_op jit(solution)/shard_map/while/body/eval_jaxpr/hqk,qhd->khd/dot_general | solution.py:214
  627.0 37.6 %multiply_reduce_fusion.5 = (f32[12,512]{1,0:T(8,128)S(1)}, f32[12,512,2048]{2,1,0:T(8,128)}) fusion(f32[12,512,2048]{2,1,0:T(8,128)} %fusion.119, f32[12,512]{1,0:T(8,128)S(1)} %dynamic-slice_bitcast_fusion.2, pred[512,2048]{1,0:T(8,128)(4,1)} %fusion.120, bf16[512,12,64]{0,2,1:T(8,128)(2,1)} %bitcast.176, bf16[2048,12,64]{0,2,1:T(8,128)(2,1)} %bitcast.169), kind=kOutput, calls=%fused_computation.21.clone.1 | convolution fusion | flops 1673521152 | bytes 105693184 | tf_op jit(solution)/shard_map/while/body/eval_jaxpr/qhd,khd->hqk/dot_general | solution.py:193
  664.6 41.4 %multiply_convert_fusion.5 = bf16[12,512,2048]{2,1,0:T(8,128)(2,1)} fusion(f32[12,512,2048]{2,1,0:T(8,128)} %get-tuple-element.712, f32[12,512,2048]{2,1,0:T(8,128)} %fusion.119, f32[12,512]{1,0:T(8,128)S(1)} %get-tuple-element.713, f32[12,512]{1,0:T(8,128)S(1)} %dynamic-slice_bitcast_fusion.2, pred[512,2048]{1,0:T(8,128)(4,1)} %fusion.120), kind=kLoop, calls=%fused_computation.20.clone.1 | loop fusion | flops 75497472 | bytes 126926848 | tf_op jit(solution)/shard_map/while/body/eval_jaxpr/convert_element_type | solution.py:195
  785.8 89.2 %reduce-scatter.9.cloned.1.call-done = f32[2,512,768]{2,1,0:T(8,128)} async-done(((f32[2,2048,768]{2,1,0:T(8,128)}), f32[2,512,768]{2,1,0:T(8,128)}) %reduce-scatter.9.cloned.1.call-update) | async-done | bytes 3145744 | tf_op jit(solution)/shard_map/reduce_scatter | solution.py:228
  877.1 121.8 %reduce-scatter.7.cloned.1.call-done = f32[2,512,768]{2,1,0:T(8,128)} async-done(((f32[2,2048,768]{2,1,0:T(8,128)}), f32[2,512,768]{2,1,0:T(8,128)}) %reduce-scatter.7.cloned.1.call-update) | async-done | bytes 3145744 | tf_op jit(solution)/shard_map/reduce_scatter | solution.py:227
  1011.6 21.2 %reduce-scatter.15.cloned.1.call-done = f32[384,3072]{1,0:T(8,128)} async-done(((f32[768,3072]{1,0:T(8,128)}), f32[384,3072]{1,0:T(8,128)}) %reduce-scatter.15.cloned.1.call-update) | async-done | bytes 4718608 | tf_op jit(solution)/shard_map/reduce_scatter | solution.py:255
  1032.8 21.5 %reduce-scatter.17.cloned.1.call-done = f32[1536,768]{1,0:T(8,128)} async-done(((f32[3072,768]{1,0:T(8,128)}), f32[1536,768]{1,0:T(8,128)}) %reduce-scatter.17.cloned.1.call-update) | async-done | bytes 4718608 | tf_op jit(solution)/shard_map/reduce_scatter | solution.py:257
  1054.3 19.1 %reduce-scatter.11.cloned.1.call-done = f32[384,2304]{1,0:T(8,128)} async-done(((f32[768,2304]{1,0:T(8,128)}), f32[384,2304]{1,0:T(8,128)}) %reduce-scatter.11.cloned.1.call-update) | async-done | bytes 3538960 | tf_op jit(solution)/shard_map/reduce_scatter | solution.py:248
  1106.9 82.5 %all-reduce.9 = (f32[384]{0:T(512)}, f32[384]{0:T(512)}, f32[384]{0:T(512)}, f32[384]{0:T(512)}, f32[384]{0:T(512)}, /*index=5*/f32[384]{0:T(512)}, f32[384]{0:T(512)}, f32[1536]{0:T(1024)}, f32[384]{0:T(512)}) all-reduce(f32[384]{0:T(512)S(1)} %dynamic-slice.11, ...), channel_id=1, replica_groups=mesh['cp'=4,'fsdp'=2,'rep'=4] {'cp','rep'}, use_global_device_ids=true, to_apply=%region_19.20 | all-reduce | flops 4608 | bytes 36864 | tf_op jit(solution)/shard_map/psum | solution.py:260
  1194.0 286.6 %all-reduce.14.cloned.1.call-done = (f32[384,2304]{1,0:T(8,128)}, f32[384,768]{1,0:T(8,128)}, f32[384,3072]{1,0:T(8,128)}, f32[1536,768]{1,0:T(8,128)}) async-done(((f32[384,2304]{1,0:T(8,128)}, f32[384,768]{1,0:T(8,128)}, f32[384,3072]{1,0:T(8,128)}, f32[1536,768]{1,0:T(8,128)}), (f32[384,2304]{1,0:T(8,128)}, f32[384,768]{1,0:T(8,128)}, f32[384,3072]{1,0:T(8,128)}, ...) | async-done | bytes 14155792 | tf_op jit(solution)/shard_map/psum | solution.py:260
  (329 shorter events, 373.0 us)
Async XLA Ops:
  7.2 17.8 %all-gather.16.cloned.1.call-start = ((), (), s32[]{:S(2)}) async-start(), calls=%async_computation.7 | async-start | bytes 5308416 | tf_op jit(solution)/shard_map/all_gather | solution.py:67
  7.9 157.3 %all-gather.18.cloned.1.call-start = ((), (), s32[]{:S(2)}) async-start(), calls=%async_computation.8 | async-start | bytes 7864320 | tf_op jit(solution)/shard_map/all_gather | solution.py:95
  34.1 298.0 %all-gather.20.cloned.1.call-start = ((), (), s32[]{:S(2)}) async-start(), calls=%async_computation.9 | async-start | bytes 1769472 | tf_op jit(solution)/shard_map/all_gather | solution.py:70
  34.8 301.7 %all-gather.22.cloned.1.call-start = ((), (), s32[]{:S(2)}) async-start(), calls=%async_computation.10 | async-start | bytes 7077888 | tf_op jit(solution)/shard_map/all_gather | solution.py:74
  35.4 312.1 %all-gather.24.cloned.1.call-start = ((), (), s32[]{:S(2)}) async-start(), calls=%async_computation.11 | async-start | bytes 7077888 | tf_op jit(solution)/shard_map/all_gather | solution.py:76
  41.0 103.3 %all-to-all-start = ((bf16[4,2,512,768]{2,3,1,0:T(8,128)(2,1)}), bf16[4,2,512,768]{2,3,1,0:T(8,128)(2,1)}, u32[]{:S(2)}, u32[]{:S(2)}) async-start(bf16[4,2,512,768]{2,3,1,0:T(8,128)(2,1)} %stack.2), calls=%async_computation | async-start | bytes 12582912 | tf_op jit(solution)/shard_map/all_to_all | solution.py:11
  46.6 332.8 %all-gather.26.cloned.1.call-start = ((), (), s32[]{:S(2)}) async-start(), calls=%async_computation.12 | async-start | bytes 7864320 | tf_op jit(solution)/shard_map/all_gather | solution.py:163
  56.4 818.6 %reduce-scatter.9.cloned.1.call-start = ((), (), s32[]{:S(2)}) async-start(), calls=%async_computation.14 | async-start | bytes 15728640 | tf_op jit(solution)/shard_map/reduce_scatter | solution.py:228
  58.1 107.2 %copy-start.24 = (s32[2,2048]{1,0:T(2,128)S(1)}, s32[2,2048]{1,0:T(2,128)}, u32[]{:S(2)}) copy-start(s32[2,2048]{1,0:T(2,128)} %param.21) | copy-start | bytes 49156
  165.3 166.9 %copy-start.47 = (f32[768]{0:T(1024)S(1)}, f32[768]{0:T(1024)}, u32[]{:S(2)}) copy-start(f32[768]{0:T(1024)} %reshape.457) | copy-start | bytes 9220
  205.6 23.9 %copy-start = (pred[512,2048]{1,0:T(8,128)(4,1)S(1)}, pred[512,2048]{1,0:T(8,128)(4,1)}, u32[]{:S(2)}) copy-start(pred[512,2048]{1,0:T(8,128)(4,1)} %fusion.105) | copy-start | bytes 3145732 | tf_op jit(solution)/shard_map/while
  205.6 23.9 %copy-start.2 = (bf16[1,2048,768]{1,2,0:T(8,128)(2,1)S(1)}, bf16[1,2048,768]{1,2,0:T(8,128)(2,1)}, u32[]{:S(2)}) copy-start(bf16[1,2048,768]{1,2,0:T(8,128)(2,1)} %constant_dynamic-slice_fusion.18) | copy-start | bytes 9437188 | tf_op jit(solution)/shard_map/while
  287.7 22.8 %copy-start.2 = (bf16[1,2048,768]{1,2,0:T(8,128)(2,1)S(1)}, bf16[1,2048,768]{1,2,0:T(8,128)(2,1)}, u32[]{:S(2)}) copy-start(bf16[1,2048,768]{1,2,0:T(8,128)(2,1)} %constant_dynamic-slice_fusion.18) | copy-start | bytes 9437188 | tf_op jit(solution)/shard_map/while
  335.9 36.6 %copy-start.6 = (f32[1024,768]{1,0:T(8,128)}, f32[1024,768]{1,0:T(8,128)S(1)}, u32[]{:S(2)}) copy-start(f32[1024,768]{1,0:T(8,128)S(1)} %get-tuple-element.571) | copy-start | bytes 9437188
  336.0 36.6 %copy-start.25 = (f32[1024]{0:T(1024)}, f32[1024]{0:T(1024)S(1)}, u32[]{:S(2)}) copy-start(f32[1024]{0:T(1024)S(1)} %broadcast_multiply_fusion) | copy-start | bytes 12292
  336.5 36.1 %copy-start.27 = (f32[1024]{0:T(1024)}, f32[1024]{0:T(1024)S(1)}, u32[]{:S(2)}) copy-start(f32[1024]{0:T(1024)S(1)} %fusion.36) | copy-start | bytes 12292
  753.4 245.5 %reduce-scatter.7.cloned.1.call-start = ((), (), s32[]{:S(2)}) async-start(), calls=%async_computation.13 | async-start | bytes 15728640 | tf_op jit(solution)/shard_map/reduce_scatter | solution.py:227
  754.2 257.4 %reduce-scatter.13.cloned.1.call-start = ((), (), s32[]{:S(2)}) async-start(), calls=%async_computation.16 | async-start | bytes 3538944 | tf_op jit(solution)/shard_map/reduce_scatter | solution.py:251
  759.1 273.7 %reduce-scatter.15.cloned.1.call-start = ((), (), s32[]{:S(2)}) async-start(), calls=%async_computation.17 | async-start | bytes 14155776 | tf_op jit(solution)/shard_map/reduce_scatter | solution.py:255
  770.9 283.4 %reduce-scatter.17.cloned.1.call-start = ((), (), s32[]{:S(2)}) async-start(), calls=%async_computation.18 | async-start | bytes 14155776 | tf_op jit(solution)/shard_map/reduce_scatter | solution.py:257
  785.5 287.9 %reduce-scatter.11.cloned.1.call-start = ((), (), s32[]{:S(2)}) async-start(), calls=%async_computation.15 | async-start | bytes 10616832 | tf_op jit(solution)/shard_map/reduce_scatter | solution.py:248
  877.0 133.4 %copy-start.16 = (bf16[2,512,768]{2,1,0:T(8,128)(2,1)}, bf16[2,512,768]{2,1,0:T(8,128)(2,1)S(1)}, u32[]{:S(2)}) copy-start(bf16[2,512,768]{2,1,0:T(8,128)(2,1)S(1)} %convert.15) | copy-start | bytes 4718596
  1010.5 470.1 %all-reduce.14.cloned.1.call-start = ((), (), s32[]{:S(2)}) async-start(), calls=%async_computation.19 | async-start | bytes 28311552 | tf_op jit(solution)/shard_map/psum | solution.py:260
  1100.6 88.8 %copy-start.40 = (f32[1024]{0:T(1024)S(1)}, f32[1024]{0:T(1024)}, u32[]{:S(2)}) copy-start(f32[1024]{0:T(1024)} %copy-done.39) | copy-start | bytes 12292
  (59 other events, 388.5 us)
Sparse Core Ops, SparseCore 0:
  9.6 15.3 all-gather.15
  34.2 130.9 all-gather.17
  166.8 9.2 all-gather.19
  177.5 15.5 all-gather.21
  194.5 15.6 all-gather.23
  212.4 71.1 all-gather.25
  753.5 121.4 reduce-scatter.8
  878.1 120.7 reduce-scatter.6
  1001.7 9.8 reduce-scatter.12
  1013.8 18.9 reduce-scatter.14
  1035.2 19.0 reduce-scatter.16
  1056.6 16.8 reduce-scatter.10
  1079.9 400.6 all-reduce.13
